TPU v7x, 128 devices: a whole 4x4x4 slice. The times are simulated.
128 devices in a mesh: belt: 16 (over x, z_lo, core), lon: 8 (over z_hi, y).
Axes of the slice: x: 4, y: 4, z: 4 (z_hi: 2, z_lo: 2; z = z_hi * 2 + z_lo), core: 2. Of those that a mesh axis runs over, the one named last changes fastest.
Arguments:
- grid_fields: bfloat16 [32, 2048, 4096], P(None, 'belt', 'lon'), may hold values from -6 to 6
- field_order: int32 [32], replicated, may hold values from 0 to 31, each once
- wave_order: int32 [1024], replicated, may hold values from 0 to 1023, as said below
Outputs:
- spectral: float32 [1024, 2, 32, 2, 512], P(('belt', 'lon'))
Inputs may be any that keep to these rules, and one draw needn't show every extreme that they name: wave_order is a permutation of the wavenumbers; each aligned block of 8 entries holds 4 wavenumbers m followed, in the same order, by their partners 1024 - 1 - m. field_order is a permutation.
All inputs are finite; a program needn't handle non-finite values.
Results may differ from a plain program's by a relative error of at most 0.0023.
Values may be sent and summed in bfloat16 or wider, within the bound.
A program may use at most 128 MiB of HBM per device.

v0:
```python
import functools
import math

import jax
import jax.numpy as jnp
from jax import lax
from jax.experimental import pallas as pl
from jax.experimental.pallas import tpu as pltpu
from jax.sharding import PartitionSpec as P

LANES = 128
LINK_DTYPE = jnp.bfloat16
NT_DIMS = (((1,), (1,)), ((), ()))


def split(value):
    high = value.astype(jnp.bfloat16)
    return high, (value - high.astype(jnp.float32)).astype(jnp.bfloat16)


def angle_factors(wavenumbers, lon_count):
    coarse = jnp.arange(lon_count // LANES, dtype=jnp.int32) * LANES
    fine = jnp.arange(LANES, dtype=jnp.int32)
    steps = jnp.concatenate((coarse, fine))
    phase = wavenumbers[:, None] * steps[None, :] % lon_count
    angles = phase.astype(jnp.float32) * (2.0 * math.pi / lon_count)
    return jnp.cos(angles), jnp.sin(angles)


def dft_table(wave_order, lon_count, slot_count):
    cosine, sine = angle_factors(wave_order, lon_count)
    coarse_count = lon_count // LANES
    pad = -coarse_count % LANES
    if pad:
        fill = ((0, 0), (0, pad))
        cosine = jnp.concatenate(
            (jnp.pad(cosine[:, :coarse_count], fill), cosine[:, coarse_count:]), axis=1
        )
        sine = jnp.concatenate(
            (jnp.pad(sine[:, :coarse_count], fill), sine[:, coarse_count:]), axis=1
        )
    owners = wave_order.shape[0] // slot_count
    width = cosine.shape[1]
    cosine = cosine.reshape(owners, slot_count, width)
    sine = sine.reshape(owners, slot_count, width)
    step = 8

    def body(cos_ref, sin_ref, out_ref):
        @pl.loop(0, step)
        def _(owner):
            cos_all = cos_ref[owner]
            sin_all = sin_ref[owner]
            cos_fine = cos_all[:, width - LANES :]
            sin_fine = sin_all[:, width - LANES :]
            row = pl.multiple_of(owner * 16, 16)
            for a in range(coarse_count):
                ca = cos_all[:, a : a + 1]
                sa = sin_all[:, a : a + 1]
                cosine_rows = ca * cos_fine - sa * sin_fine
                sine_rows = sa * cos_fine + ca * sin_fine
                out_ref[pl.ds(row, 16), a * LANES : (a + 1) * LANES] = jnp.concatenate(
                    (cosine_rows, -sine_rows), axis=0
                ).astype(jnp.bfloat16)

    return pl.pallas_call(
        body,
        name="dft_table",
        grid=(owners // step,),
        in_specs=[pl.BlockSpec((step, slot_count, width), lambda i: (i, 0, 0))] * 2,
        out_specs=pl.BlockSpec((step * 16, lon_count), lambda i: (i, 0)),
        out_shape=jax.ShapeDtypeStruct((owners * 16, lon_count), jnp.bfloat16),
        cost_estimate=pl.CostEstimate(
            flops=owners * 16 * lon_count * 4, bytes_accessed=owners * 32 * lon_count, transcendentals=0
        ),
    )(cosine, sine)


def dft(table, samples, scale):
    parts, rows, length = samples.shape
    table_rows = table.shape[0]
    step = 512

    def body(table_ref, samples_ref, out_ref):
        total = None
        for part in range(parts):
            term = lax.dot_general(
                table_ref[:, part * length : (part + 1) * length],
                samples_ref[part],
                NT_DIMS,
                preferred_element_type=jnp.float32,
            )
            total = term if total is None else total + term
        out_ref[...] = (total * scale).astype(out_ref.dtype)

    return pl.pallas_call(
        body,
        name="dft",
        grid=(table_rows // step,),
        in_specs=[
            pl.BlockSpec((step, parts * length), lambda i: (i, 0)),
            pl.BlockSpec((parts, rows, length), lambda i: (0, 0, 0)),
        ],
        out_specs=pl.BlockSpec((step, rows), lambda i: (i, 0)),
        out_shape=jax.ShapeDtypeStruct((table_rows, rows), LINK_DTYPE),
        compiler_params=pltpu.CompilerParams(vmem_limit_bytes=48 << 20),
        cost_estimate=pl.CostEstimate(
            flops=2 * table_rows * rows * parts * length,
            bytes_accessed=2 * table_rows * parts * length,
            transcendentals=0,
        ),
    )(table, samples)


def latitude_geometry(lat_count):
    lat_index = jnp.arange(lat_count // 2).astype(jnp.float32)
    colatitude = math.pi * (lat_index + 0.75) / (lat_count + 0.5)
    sine_lat = jnp.sin(colatitude)
    weight = math.pi / (lat_count + 0.5) * sine_lat * math.sqrt(lat_count / 2.0)
    return (jnp.cos(colatitude), sine_lat, weight)


def legendre(wavenumbers, mode_count, lat_count):
    slots = wavenumbers.shape[0]
    half = lat_count // 2
    chunks = half // LANES
    wave_value = wavenumbers.astype(jnp.float32)[:, None]
    cosine, sine_lat, weight = latitude_geometry(lat_count)
    term_index = jnp.arange(1, mode_count + 1).astype(jnp.float32)
    log_terms = jnp.log1p(0.5 / term_index)
    start_sum = jnp.sum(
        jnp.where(term_index[None, :] <= wave_value, log_terms[None, :], 0.0), axis=1, keepdims=True
    )
    log_start = -0.5 * math.log(2.0) + 0.5 * start_sum + wave_value * jnp.log(sine_lat)[None, :]
    geometry = jnp.stack((cosine, weight))[:, None, :] * jnp.ones((2, slots, 1), jnp.float32)
    wave_lanes = jnp.broadcast_to(wave_value, (slots, LANES))
    block = 32
    renorm = 16

    def body(wave_ref, log_ref, geo_ref, out_ref, prev_ref, cur_ref, scale_ref, inv_ref, rows_ref):
        step = pl.program_id(0)

        @pl.when(step == 0)
        def _():
            prev_ref[...] = jnp.zeros_like(prev_ref)
            cur_ref[...] = jnp.ones_like(cur_ref)
            scale_ref[...] = log_ref[...]
            inv_ref[...] = jnp.zeros_like(inv_ref)

        wave = wave_ref[...]
        first = (step * block).astype(jnp.float32)
        lanes = [slice(a * LANES, (a + 1) * LANES) for a in range(chunks)]
        inverse = inv_ref[...]
        prev = [prev_ref[:, s] for s in lanes]
        cur = [cur_ref[:, s] for s in lanes]
        amp = [None] * chunks
        for row in range(block):
            if row % renorm == 0:
                for a in range(chunks):
                    total = jnp.maximum(jnp.abs(prev[a]) + jnp.abs(cur[a]), 1e-30)
                    prev[a] = prev[a] / total
                    cur[a] = cur[a] / total
                    log_scale = scale_ref[:, lanes[a]] + jnp.log(total)
                    scale_ref[:, lanes[a]] = log_scale
                    amp[a] = jnp.exp(log_scale) * geo_ref[1, :, lanes[a]]
            for a in range(chunks):
                rows_ref[a, row * slots : (row + 1) * slots, :] = cur[a] * amp[a]
            offset = first + (row + 1.0)
            degree = wave + offset
            numer = 4.0 * degree * degree - 1.0
            denom = offset * (wave + degree)
            root = lax.rsqrt(numer * denom)
            keep = degree < mode_count
            factor = jnp.where(keep, numer * root, 0.0)
            ratio = factor * inverse
            inverse = denom * root
            for a in range(chunks):
                following = (factor * geo_ref[0, :, lanes[a]]) * cur[a] - ratio * prev[a]
                prev[a] = cur[a]
                cur[a] = following
        inv_ref[...] = inverse
        for a in range(chunks):
            prev_ref[:, lanes[a]] = prev[a]
            cur_ref[:, lanes[a]] = cur[a]
        for slot in range(slots):
            for parity in range(2):
                for a in range(chunks):
                    value = rows_ref[a, pl.ds(parity * slots + slot, block // 2, stride=2 * slots), :]
                    high, low = split(value)
                    out_ref[slot, parity, 0, :, lanes[a]] = high
                    out_ref[slot, parity, 1, :, lanes[a]] = low

    return pl.pallas_call(
        body,
        name="legendre",
        grid=(mode_count // block,),
        in_specs=[
            pl.BlockSpec((slots, LANES), lambda i: (0, 0)),
            pl.BlockSpec((slots, half), lambda i: (0, 0)),
            pl.BlockSpec((2, slots, half), lambda i: (0, 0, 0)),
        ],
        out_specs=pl.BlockSpec((slots, 2, 2, block // 2, half), lambda i: (0, 0, 0, i, 0)),
        out_shape=jax.ShapeDtypeStruct((slots, 2, 2, mode_count // 2, half), jnp.bfloat16),
        scratch_shapes=[
            pltpu.VMEM((slots, half), jnp.float32),
            pltpu.VMEM((slots, half), jnp.float32),
            pltpu.VMEM((slots, half), jnp.float32),
            pltpu.VMEM((slots, LANES), jnp.float32),
            pltpu.VMEM((chunks, block * slots, LANES), jnp.float32),
        ],
        cost_estimate=pl.CostEstimate(
            flops=slots * half * mode_count * 10,
            bytes_accessed=slots * half * mode_count * 4,
            transcendentals=0,
        ),
    )(wave_lanes, log_start, geometry)


def project(received, legendre_table, field_order, belts, lons):
    slots, _, _, half_modes, half = legendre_table.shape
    sources = belts * lons
    lat_local = 2 * half // belts
    items = received.shape[2] // lat_local
    levels = items * lons
    rows = 2 * levels
    level_of = field_order.astype(jnp.int32)
    target = jnp.arange(2 * rows, dtype=jnp.int32)
    within = target % rows
    source_level = jnp.take(level_of, within % levels)
    source_row = (source_level % items) * (2 * lons) + (source_level // items) * 2 + within // levels
    source_row = source_row + (target // rows) * rows
    order = (source_row[:, None] == jnp.arange(2 * rows, dtype=jnp.int32)[None, :]).astype(jnp.bfloat16)
    mirror = (
        jnp.arange(lat_local)[:, None] + jnp.arange(lat_local)[None, :] == lat_local - 1
    ).astype(jnp.bfloat16)

    def body(received_ref, table_ref, order_ref, mirror_ref, out_ref, wide_ref, sums_ref):
        slot = pl.program_id(0)
        parity = pl.program_id(1)

        @pl.when((slot == 0) & (parity == 0))
        def _():
            @pl.loop(0, belts)
            def _(belt):
                for lon in range(lons):
                    value = received_ref[belt * lons + lon].astype(jnp.float32)
                    for item in range(items):
                        wide_ref[belt, item, lon * 2 * slots : (lon + 1) * 2 * slots, :] = value[
                            :, item * lat_local : (item + 1) * lat_local
                        ]

        @pl.when(parity == 0)
        def _():
            def rows_of(belt):
                return jnp.concatenate(
                    [wide_ref[belt, item, pl.ds(slot, 2 * lons, stride=slots), :] for item in range(items)],
                    axis=0,
                )

            for belt in range(belts // 2):
                north = rows_of(belt)
                south = jnp.dot(
                    rows_of(belts - 1 - belt).astype(LINK_DTYPE),
                    mirror_ref[...],
                    preferred_element_type=jnp.float32,
                )
                for index, value in enumerate((north + south, north - south)):
                    ordered = jnp.dot(
                        order_ref[...],
                        jnp.concatenate(split(value), axis=0),
                        preferred_element_type=jnp.float32,
                    )
                    sums_ref[index, :, belt * lat_local : (belt + 1) * lat_local] = ordered.astype(jnp.bfloat16)

        result = lax.dot_general(
            sums_ref[parity], table_ref[0, 0, 0], NT_DIMS, preferred_element_type=jnp.float32
        ) + lax.dot_general(
            sums_ref[parity], table_ref[0, 0, 1], NT_DIMS, preferred_element_type=jnp.float32
        )
        out_ref[0] = result[:rows] + result[rows:]

    return pl.pallas_call(
        body,
        name="project",
        grid=(slots, 2),
        in_specs=[
            pl.BlockSpec(received.shape, lambda s, p: (0, 0, 0)),
            pl.BlockSpec((1, 1, 2, half_modes, half), lambda s, p: (s, p, 0, 0, 0)),
            pl.BlockSpec((2 * rows, 2 * rows), lambda s, p: (0, 0)),
            pl.BlockSpec((lat_local, lat_local), lambda s, p: (0, 0)),
        ],
        out_specs=pl.BlockSpec((1, rows, half_modes), lambda s, p: (s, 0, p)),
        out_shape=jax.ShapeDtypeStruct((slots, rows, 2 * half_modes), jnp.float32),
        scratch_shapes=[
            pltpu.VMEM((belts, items, 2 * lons * slots, lat_local), jnp.float32),
            pltpu.VMEM((2, 2 * rows, half), jnp.bfloat16),
        ],
        compiler_params=pltpu.CompilerParams(vmem_limit_bytes=40 << 20),
    )(received, legendre_table, order, mirror)


def on_device(grid_fields, field_order, wave_order):
    belts = lax.axis_size("belt")
    lons = lax.axis_size("lon")
    levels, lat_local, lon_local = grid_fields.shape
    lat_count = lat_local * belts
    lon_count = lon_local * lons
    mode_count = wave_order.shape[0]
    slots = mode_count // (belts * lons)
    items = levels // lons
    blocks = grid_fields.reshape(lons, items * lat_local, lon_local)
    gathered = lax.all_to_all(blocks, "lon", split_axis=0, concat_axis=0, tiled=True)
    table = dft_table(wave_order, lon_count, slots)
    owner = lax.axis_index("belt") * lons + lax.axis_index("lon")
    own_waves = lax.dynamic_slice_in_dim(wave_order, owner * slots, slots, 0)
    legendre_table = legendre(own_waves, mode_count, lat_count)
    fourier = dft(table, gathered, 1.0 / math.sqrt(lon_count))
    fourier = fourier.reshape(belts * lons, 2 * slots, items * lat_local)
    received = lax.all_to_all(fourier, ("belt", "lon"), split_axis=0, concat_axis=0, tiled=True)
    spectral = project(received, legendre_table, field_order, belts, lons)
    return spectral.reshape(slots, 2, levels, 2, mode_count // 2)


def solution(mesh):
    return jax.shard_map(
        on_device,
        mesh=mesh,
        in_specs=(P(None, "belt", "lon"), P(), P()),
        out_specs=P(("belt", "lon"), None, None, None, None),
        check_vma=False,
    )
```

profile of v0, /device:TPU:1, one launch (start us, length us, event | category | flops | bytes accessed | tf_op | source)
XLA Modules:
  0.0 163.6 jit_solution(6881643171785812913)
XLA Ops:
  0.0 0.0 copy-start
  0.0 0.0 copy-start.4
  0.0 8.5 %all-to-all-start = ((bf16[8,512,512]{2,1,0:T(8,128)(2,1)}), bf16[8,512,512]{2,1,0:T(8,128)(2,1)}, u32[]{:S(2)}, u32[]{:S(2)}) async-start(bf16[8,512,512]{2,1,0:T(8,128)(2,1)} %bitcast.9), calls=%async_computation | async-start | bytes 8388608 | tf_op jit(solution)/shard_map/all_to_all | solution.py:311
  8.5 0.1 pad_add_fusion
  8.6 0.0 copy-done.4
  8.6 4.1 %fusion.3 = (f32[1024,160]{1,0:T(8,128)S(1)}, f32[1024,160]{1,0:T(8,128)S(1)}) fusion(s32[160]{0:T(256)S(1)} %pad_add_fusion, s32[1024]{0:T(1024)S(1)} %copy-done.4), kind=kLoop, calls=%fused_computation.13 | loop fusion | flops 2293760 | bytes 1315456 | tf_op jit(solution)/shard_map/sin | solution.py:27
  12.7 0.0 copy-done.5
  12.7 0.4 slice_select_fusion
  13.1 1.4 maximum_bitcast_fusion
  14.5 24.6 %dft_table.1.table_ref = bf16[2048,4096]{1,0:T(8,128)(2,1)} custom-call(f32[128,8,256]{2,1,0:T(8,128)} %get-tuple-element.13.cos_ref, f32[128,8,256]{2,1,0:T(8,128)} %get-tuple-element.14.sin_ref), custom_call_target="tpu_custom_call" | custom-call | flops 33554432 | bytes 16777216 | tf_op jit(solution)/shard_map/dft_table/pallas_call | solution.py:65
  39.2 20.5 %all-to-all-done.samples_ref = bf16[8,512,512]{2,1,0:T(8,128)(2,1)} async-done(((bf16[8,512,512]{2,1,0:T(8,128)(2,1)}), bf16[8,512,512]{2,1,0:T(8,128)(2,1)}, u32[]{:S(2)}, u32[]{:S(2)}) %all-to-all-start) | async-done | bytes 4194336 | tf_op jit(solution)/shard_map/all_to_all | solution.py:311
  59.7 13.0 %dft.1 = bf16[2048,512]{1,0:T(8,128)(2,1)S(1)} custom-call(bf16[2048,4096]{1,0:T(8,128)(2,1)} %dft_table.1.table_ref, bf16[8,512,512]{2,1,0:T(8,128)(2,1)} %all-to-all-done.samples_ref), custom_call_target="tpu_custom_call" | custom-call | flops 8589934592 | bytes 16777216 | tf_op jit(solution)/shard_map/dft/pallas_call | solution.py:95
  72.6 0.0 copy-start.3
  72.6 1.3 copy-done.3
  74.0 20.1 %all-to-all-start.1 = ((bf16[128,16,512]{2,1,0:T(8,128)(2,1)}), bf16[128,16,512]{2,1,0:T(8,128)(2,1)S(1)}, u32[]{:S(2)}, u32[]{:S(2)}) async-start(bf16[128,16,512]{2,1,0:T(8,128)(2,1)} %bitcast.8), calls=%async_computation.1 | async-start | bytes 4194304 | tf_op jit(solution)/shard_map/all_to_all | solution.py:318
  94.1 0.0 copy-done
  94.1 1.2 gather_fusion
  95.4 0.1 dynamic-slice_convert_fusion
  95.5 0.1 sine_multiply_fusion
  95.7 0.2 select_reduce_fusion
  95.9 0.7 multiply_add_fusion.log_ref
  96.6 0.7 broadcast_in_dim.18.wave_ref
  97.2 0.6 mul.112.geo_ref
  97.9 28.2 %legendre.1.table_ref = bf16[8,2,2,512,1024]{4,3,2,1,0:T(8,128)(2,1)} custom-call(f32[8,128]{1,0:T(8,128)} %broadcast_in_dim.18.wave_ref, f32[8,1024]{1,0:T(8,128)} %multiply_add_fusion.log_ref, f32[2,8,1024]{2,1,0:T(8,128)} %mul.112.geo_ref), custom_call_target="tpu_custom_call" | custom-call | flops 83886080 | bytes 33554432 | tf_op jit(solution)/shard_map/legendre/pallas_call | solution.py:192
  126.1 0.1 fusion.5
  126.2 0.0 all-to-all-done.1.received_ref
  126.2 0.0 copy-start.1
  126.2 32.0 %project.1 = f32[8,64,1024]{2,1,0:T(8,128)S(1)} custom-call(bf16[128,16,512]{2,1,0:T(8,128)(2,1)S(1)} %all-to-all-done.1.received_ref, bf16[8,2,2,512,1024]{4,3,2,1,0:T(8,128)(2,1)} %legendre.1.table_ref, bf16[128,128]{1,0:T(8,128)(2,1)S(1)} %get-tuple-element.17.order_ref, bf16[128,128]{1,0:T(8,128)(2,1)S(1)} %get-tuple-element.18.mirror_ref), custom_call_target="tpu_custom_call" | custom-call | tf_op jit(solution)/shard_map/project/pallas_call | solution.py:281
  158.3 0.0 copy-start.2
  158.3 1.3 copy-done.2
  159.6 4.0 %reshape.199 = f32[8,2,32,2,512]{4,3,2,1,0:T(2,128)} reshape(f32[8,64,1024]{2,1,0:T(8,128)} %copy-done.2) | data formatting | bytes 4194304 | tf_op jit(solution)/shard_map/reshape | solution.py:320
  163.6 0.0 copy-done.1
  (11 shorter events, 0.1 us)
Async XLA Ops:
  0.0 94.1 %copy-start = (s32[32]{0:T(128)S(1)}, s32[32]{0:T(128)}, u32[]{:S(2)}) copy-start(s32[32]{0:T(128)} %param.4) | copy-start | bytes 388
  0.0 8.6 %copy-start.4 = (s32[1024]{0:T(1024)S(1)}, s32[1024]{0:T(1024)}, u32[]{:S(2)}) copy-start(s32[1024]{0:T(1024)} %param.5) | copy-start | bytes 12292
  0.0 12.7 %copy-start.5 = (pred[128]{0:T(512)(128)(4,1)S(1)}, pred[128]{0:T(512)(128)(4,1)}, u32[]{:S(2)}) copy-start(pred[128]{0:T(512)(128)(4,1)} %constant.114.clone.1) | copy-start | bytes 388
  0.0 59.6 %all-to-all-start = ((bf16[8,512,512]{2,1,0:T(8,128)(2,1)}), bf16[8,512,512]{2,1,0:T(8,128)(2,1)}, u32[]{:S(2)}, u32[]{:S(2)}) async-start(bf16[8,512,512]{2,1,0:T(8,128)(2,1)} %bitcast.9), calls=%async_computation | async-start | bytes 8388608 | tf_op jit(solution)/shard_map/all_to_all | solution.py:311
  72.6 1.3 copy-start.3
  74.0 52.2 %all-to-all-start.1 = ((bf16[128,16,512]{2,1,0:T(8,128)(2,1)}), bf16[128,16,512]{2,1,0:T(8,128)(2,1)S(1)}, u32[]{:S(2)}, u32[]{:S(2)}) async-start(bf16[128,16,512]{2,1,0:T(8,128)(2,1)} %bitcast.8), calls=%async_computation.1 | async-start | bytes 4194304 | tf_op jit(solution)/shard_map/all_to_all | solution.py:318
  126.2 37.4 %copy-start.1 = (s32[32]{0:T(128)S(1)}, s32[32]{0:T(128)}, u32[]{:S(2)}) copy-start(s32[32]{0:T(128)} %param.4) | copy-start | bytes 388
  158.3 1.3 copy-start.2
where the time goes:
time: 164 us
  Pallas kernels  97.8 us (60%)
  starting transfers between devices  28.6 us (17%)
  waiting for transfers between devices  20.5 us (12%)
  local copies, waits for them, and re-layouts  9.15 us (6%)
  other arithmetic  7.33 us (4%)
    pallas_call x1, Pallas kernels, project(): pl.pallas_call(body, name='project', grid=(slots, 2), in_specs=[pl.BlockS...  32 us
    pallas_call x1, Pallas kernels, legendre(): pl.pallas_call(body, name='legendre', grid=(mode_count // block,), in_spe...  28.2 us
    pallas_call x1, Pallas kernels, dft_table(): pl.pallas_call(body, name='dft_table', grid=(owners // step,), in_specs=[...  24.6 us
    all_to_all x1, waiting for transfers between devices, on_device(): lax.all_to_all(blocks, 'lon', split_axis=0, concat_axis=0, tiled=True)  20.5 us
    all_to_all x1, starting transfers between devices, on_device(): lax.all_to_all(fourier, ('belt', 'lon'), split_axis=0, concat_axis=0, til...  20.1 us
    pallas_call x1, Pallas kernels, dft(): pl.pallas_call(body, name='dft', grid=(table_rows // step,), in_specs=[pl...  13 us
    all_to_all x1, starting transfers between devices, on_device(): lax.all_to_all(blocks, 'lon', split_axis=0, concat_axis=0, tiled=True)  8.46 us
    sin x1, other arithmetic, angle_factors(): return (jnp.cos(angles), jnp.sin(angles))  4.15 us
  transfers between devices with their start and end apart: 2, of which 1 were waited for; matrix products, arithmetic and copies ran while one was open for 6% of the time, Pallas kernels for 32%

commit v1 on v0

--- a/solution.py
+++ b/solution.py
@@ -75,38 +75,127 @@
     )(cosine, sine)
 
 
-def dft(table, samples, scale):
+def transform_and_exchange(table, samples, scale):
+    belts = lax.axis_size("belt")
+    lons = lax.axis_size("lon")
     parts, rows, length = samples.shape
-    table_rows = table.shape[0]
-    step = 512
-
-    def body(table_ref, samples_ref, out_ref):
-        total = None
-        for part in range(parts):
-            term = lax.dot_general(
-                table_ref[:, part * length : (part + 1) * length],
-                samples_ref[part],
-                NT_DIMS,
-                preferred_element_type=jnp.float32,
+    owners = belts * lons
+    group = 2 * lons
+    blocks = owners // group
+    owner_rows = table.shape[0] // owners
+    block_rows = group * owner_rows
+    mesh_id = pl.DeviceIdType.MESH
+
+    def body(table_ref, samples_ref, out_ref, stage_ref, send_ref, stage_sem, send_sem, recv_sem, local_sem):
+        belt = lax.axis_index("belt")
+        lon = lax.axis_index("lon")
+        me = belt * lons + lon
+        barrier = pltpu.get_barrier_semaphore()
+
+        def place(step):
+            away = blocks - 1 - step
+            x = lax.rem(belt // 4 + away // 2, blocks // 2)
+            return x * 2 + lax.rem(lax.rem(belt // 2, 2) + lax.rem(away, 2), 2)
+
+        def member(index):
+            away = lax.rem(index, lons)
+            core = lax.rem(lax.rem(belt, 2) + index // lons, 2)
+            half = lons // 2
+            high = lax.rem(lon // half + away // half, 2)
+            return core, high * half + lax.rem(lax.rem(lon, half) + lax.rem(away, half), half)
+
+        def fetch(step, slot):
+            return pltpu.make_async_copy(
+                table_ref.at[pl.ds(pl.multiple_of(place(step) * block_rows, block_rows), block_rows)],
+                stage_ref.at[slot],
+                stage_sem.at[slot],
             )
-            total = term if total is None else total + term
-        out_ref[...] = (total * scale).astype(out_ref.dtype)
+
+        def send(step, index):
+            core, target = member(index)
+            return pltpu.make_async_remote_copy(
+                send_ref.at[step, core * lons + target],
+                out_ref.at[me],
+                send_sem,
+                recv_sem,
+                device_id=(place(step) * 2 + core, target),
+                device_id_type=mesh_id,
+            )
+
+        fetch(0, 0).start()
+
+        @pl.loop(1, owners)
+        def _(away):
+            peer = lax.rem(me + away, owners)
+            pl.semaphore_signal(
+                barrier, inc=1, device_id=(peer // lons, lax.rem(peer, lons)), device_id_type=mesh_id
+            )
+
+        @pl.loop(0, blocks)
+        def _(step):
+            slot = lax.rem(step, 2)
+            fetch(step, slot).wait()
+
+            @pl.when(step < blocks - 1)
+            def _():
+                fetch(step + 1, 1 - slot).start()
+
+            total = None
+            for part in range(parts):
+                term = lax.dot_general(
+                    stage_ref[slot, :, part * length : (part + 1) * length],
+                    samples_ref[part],
+                    NT_DIMS,
+                    preferred_element_type=jnp.float32,
+                )
+                total = term if total is None else total + term
+            send_ref[step] = (total * scale).astype(LINK_DTYPE).reshape(group, owner_rows, rows)
+
+            @pl.when(step == 0)
+            def _():
+                pl.semaphore_wait(barrier, owners - 1)
+
+            @pl.loop(0, group)
+            def _(back):
+                index = group - 1 - back
+
+                @pl.when((step < blocks - 1) | (index > 0))
+                def _():
+                    send(step, index).start()
+
+        core, target = member(0)
+        local = pltpu.make_async_copy(
+            send_ref.at[blocks - 1, core * lons + target], out_ref.at[me], local_sem
+        )
+        local.start()
+        local.wait()
+        everything = pltpu.make_async_remote_copy(
+            out_ref.at[pl.ds(0, owners - 1)],
+            out_ref.at[pl.ds(0, owners - 1)],
+            send_sem,
+            recv_sem,
+            device_id=(lax.rem(belt + 1, belts), lon),
+            device_id_type=mesh_id,
+        )
+        everything.wait_recv()
+        everything.wait_send()
 
     return pl.pallas_call(
         body,
-        name="dft",
-        grid=(table_rows // step,),
-        in_specs=[
-            pl.BlockSpec((step, parts * length), lambda i: (i, 0)),
-            pl.BlockSpec((parts, rows, length), lambda i: (0, 0, 0)),
+        name="transform_and_exchange",
+        in_specs=[pl.BlockSpec(memory_space=pl.ANY), pl.BlockSpec(memory_space=pltpu.VMEM)],
+        out_specs=pl.BlockSpec(memory_space=pl.ANY),
+        out_shape=jax.ShapeDtypeStruct((owners, owner_rows, rows), LINK_DTYPE),
+        scratch_shapes=[
+            pltpu.VMEM((2, block_rows, parts * length), jnp.bfloat16),
+            pltpu.VMEM((blocks, group, owner_rows, rows), LINK_DTYPE),
+            pltpu.SemaphoreType.DMA((2,)),
+            pltpu.SemaphoreType.DMA,
+            pltpu.SemaphoreType.DMA,
+            pltpu.SemaphoreType.DMA,
         ],
-        out_specs=pl.BlockSpec((step, rows), lambda i: (i, 0)),
-        out_shape=jax.ShapeDtypeStruct((table_rows, rows), LINK_DTYPE),
-        compiler_params=pltpu.CompilerParams(vmem_limit_bytes=48 << 20),
-        cost_estimate=pl.CostEstimate(
-            flops=2 * table_rows * rows * parts * length,
-            bytes_accessed=2 * table_rows * parts * length,
-            transcendentals=0,
+        compiler_params=pltpu.CompilerParams(
+            collective_id=0, has_side_effects=True, vmem_limit_bytes=40 << 20
         ),
     )(table, samples)
 
@@ -313,9 +402,8 @@
     owner = lax.axis_index("belt") * lons + lax.axis_index("lon")
     own_waves = lax.dynamic_slice_in_dim(wave_order, owner * slots, slots, 0)
     legendre_table = legendre(own_waves, mode_count, lat_count)
-    fourier = dft(table, gathered, 1.0 / math.sqrt(lon_count))
-    fourier = fourier.reshape(belts * lons, 2 * slots, items * lat_local)
-    received = lax.all_to_all(fourier, ("belt", "lon"), split_axis=0, concat_axis=0, tiled=True)
+    table, legendre_table = lax.optimization_barrier((table, legendre_table))
+    received = transform_and_exchange(table, gathered, 1.0 / math.sqrt(lon_count))
     spectral = project(received, legendre_table, field_order, belts, lons)
     return spectral.reshape(slots, 2, levels, 2, mode_count // 2)
 

time: 164 us -> 148 us (0.902)
  Pallas kernels: 97.8 us -> 126 us
  waiting for transfers between devices: 20.5 us -> 0.01 us
  starting transfers between devices: 28.6 us -> 8.46 us
  local copies, waits for them, and re-layouts: 9.15 us -> 5.32 us
    pallas_call x1, Pallas kernels: 13 us -> 41.1 us  [transform_and_exchange(): pl.pallas_call(body, name='transform_and_exchange', in_specs=[pl.BlockSpe...]
    all_to_all x1, waiting for transfers between devices: 20.5 us -> 0.01 us  [on_device(): lax.all_to_all(blocks, 'lon', split_axis=0, concat_axis=0, tiled=True)]
    all_to_all x1 -> x0, starting transfers between devices: 20.1 us -> none  [on_device(): lax.all_to_all(fourier, ('belt', 'lon'), split_axis=0, concat_axis=0, til...]
    unnamed x12 -> x8, local copies, waits for them, and re-layouts: 2.66 us -> 0.02 us
  transfers between devices with their start and end apart: 2 -> 1, of which waited for: 1 -> 0; matrix products, arithmetic and copies ran while one was open for 6% -> 7% of each run, Pallas kernels for 32% -> 36%
where the time goes in v1:
time: 148 us; the launch traced here: 147 us
  Pallas kernels  126 us (85%)
  starting transfers between devices  8.46 us (6%)
  other arithmetic  7.32 us (5%)
  local copies, waits for them, and re-layouts  5.32 us (4%)
    pallas_call x1, Pallas kernels, transform_and_exchange(): pl.pallas_call(body, name='transform_and_exchange', in_specs=[pl.BlockSpe...  41.1 us
    pallas_call x1, Pallas kernels, project(): pl.pallas_call(body, name='project', grid=(slots, 2), in_specs=[pl.BlockS...  32.1 us
    pallas_call x1, Pallas kernels, legendre(): pl.pallas_call(body, name='legendre', grid=(mode_count // block,), in_spe...  28.2 us
    pallas_call x1, Pallas kernels, dft_table(): pl.pallas_call(body, name='dft_table', grid=(owners // step,), in_specs=[...  24.6 us
    all_to_all x1, starting transfers between devices, on_device(): lax.all_to_all(blocks, 'lon', split_axis=0, concat_axis=0, tiled=True)  8.46 us
    sin x1, other arithmetic, angle_factors(): return (jnp.cos(angles), jnp.sin(angles))  4.15 us
  transfers between devices with their start and end apart: 1, of which 0 were waited for; matrix products, arithmetic and copies ran while one was open for 7% of the time, Pallas kernels for 36%

profile of v1, /device:TPU:1, one launch (start us, length us, event | category | flops | bytes accessed | tf_op | source)
XLA Modules:
  0.0 147.2 jit_solution(1623707513114831368)
XLA Ops:
  0.0 0.0 copy-start
  0.0 0.0 copy-start.2
  0.0 0.0 copy-start.3
  0.0 8.5 %all-to-all-start = ((bf16[8,512,512]{2,1,0:T(8,128)(2,1)}), bf16[8,512,512]{2,1,0:T(8,128)(2,1)}, u32[]{:S(2)}, u32[]{:S(2)}) async-start(bf16[8,512,512]{2,1,0:T(8,128)(2,1)} %bitcast.7), calls=%async_computation | async-start | bytes 8388608 | tf_op jit(solution)/shard_map/all_to_all | solution.py:400
  8.5 0.1 pad_add_fusion
  8.6 0.0 copy-done.2
  8.6 4.1 %fusion.3 = (f32[1024,160]{1,0:T(8,128)S(1)}, f32[1024,160]{1,0:T(8,128)S(1)}) fusion(s32[160]{0:T(256)S(1)} %pad_add_fusion, s32[1024]{0:T(1024)S(1)} %copy-done.2), kind=kLoop, calls=%fused_computation.13 | loop fusion | flops 2293760 | bytes 1315456 | tf_op jit(solution)/shard_map/sin | solution.py:27
  12.7 0.0 copy-done.3
  12.7 0.4 slice_select_fusion
  13.1 1.4 maximum_bitcast_fusion
  14.5 24.6 %dft_table.1.table_ref = bf16[2048,4096]{1,0:T(8,128)(2,1)} custom-call(f32[128,8,256]{2,1,0:T(8,128)} %get-tuple-element.17.cos_ref, f32[128,8,256]{2,1,0:T(8,128)} %get-tuple-element.18.sin_ref), custom_call_target="tpu_custom_call" | custom-call | flops 33554432 | bytes 16777216 | tf_op jit(solution)/shard_map/dft_table/pallas_call | solution.py:65
  39.2 0.1 dynamic-slice_convert_fusion
  39.3 0.1 sine_multiply_fusion
  39.5 0.2 select_reduce_fusion
  39.7 0.7 multiply_add_fusion.log_ref
  40.4 0.7 broadcast_in_dim.18.wave_ref
  41.0 0.6 mul.112.geo_ref
  41.7 28.2 %legendre.1.table_ref = bf16[8,2,2,512,1024]{4,3,2,1,0:T(8,128)(2,1)} custom-call(f32[8,128]{1,0:T(8,128)} %broadcast_in_dim.18.wave_ref, f32[8,1024]{1,0:T(8,128)} %multiply_add_fusion.log_ref, f32[2,8,1024]{2,1,0:T(8,128)} %mul.112.geo_ref), custom_call_target="tpu_custom_call" | custom-call | flops 83886080 | bytes 33554432 | tf_op jit(solution)/shard_map/legendre/pallas_call | solution.py:281
  69.9 0.0 copy-done
  69.9 1.2 gather_fusion
  71.2 0.1 fusion.5
  71.3 0.0 all-to-all-done.samples_ref
  71.3 41.1 %transform_and_exchange.1.received_ref = bf16[128,16,512]{2,1,0:T(8,128)(2,1)S(1)} custom-call(bf16[2048,4096]{1,0:T(8,128)(2,1)} %dft_table.1.table_ref, bf16[8,512,512]{2,1,0:T(8,128)(2,1)} %all-to-all-done.samples_ref), custom_call_target="tpu_custom_call" | custom-call | tf_op jit(solution)/shard_map/transform_and_exchange/pallas_call | solution.py:183
  112.4 0.0 copy-start.1
  112.4 32.1 %project.1 = f32[8,64,1024]{2,1,0:T(8,128)S(1)} custom-call(bf16[128,16,512]{2,1,0:T(8,128)(2,1)S(1)} %transform_and_exchange.1.received_ref, bf16[8,2,2,512,1024]{4,3,2,1,0:T(8,128)(2,1)} %legendre.1.table_ref, bf16[128,128]{1,0:T(8,128)(2,1)S(1)} %get-tuple-element.21.order_ref, bf16[128,128]{1,0:T(8,128)(2,1)S(1)} %get-tuple-element.22.mirror_ref), custom_call_target="tpu_custom_call" | custom-call | tf_op jit(solution)/shard_map/project/pallas_call | solution.py:370
  144.5 2.8 %reshape.195 = f32[8,2,32,2,512]{4,3,2,1,0:T(2,128)} reshape(f32[8,64,1024]{2,1,0:T(8,128)S(1)} %project.1) | data formatting | bytes 4194304 | tf_op jit(solution)/shard_map/reshape | solution.py:408
  147.2 0.0 copy-done.1
  (10 shorter events, 0.1 us)
Async XLA Ops:
  0.0 69.9 %copy-start = (s32[32]{0:T(128)S(1)}, s32[32]{0:T(128)}, u32[]{:S(2)}) copy-start(s32[32]{0:T(128)} %param.4) | copy-start | bytes 388
  0.0 8.6 %copy-start.2 = (s32[1024]{0:T(1024)S(1)}, s32[1024]{0:T(1024)}, u32[]{:S(2)}) copy-start(s32[1024]{0:T(1024)} %param.5) | copy-start | bytes 12292
  0.0 12.7 %copy-start.3 = (pred[128]{0:T(512)(128)(4,1)S(1)}, pred[128]{0:T(512)(128)(4,1)}, u32[]{:S(2)}) copy-start(pred[128]{0:T(512)(128)(4,1)} %constant.114.clone.1) | copy-start | bytes 388
  0.0 71.2 %all-to-all-start = ((bf16[8,512,512]{2,1,0:T(8,128)(2,1)}), bf16[8,512,512]{2,1,0:T(8,128)(2,1)}, u32[]{:S(2)}, u32[]{:S(2)}) async-start(bf16[8,512,512]{2,1,0:T(8,128)(2,1)} %bitcast.7), calls=%async_computation | async-start | bytes 8388608 | tf_op jit(solution)/shard_map/all_to_all | solution.py:400
  112.4 34.9 %copy-start.1 = (s32[32]{0:T(128)S(1)}, s32[32]{0:T(128)}, u32[]{:S(2)}) copy-start(s32[32]{0:T(128)} %param.4) | copy-start | bytes 388

commit v2 on v1

--- a/solution.py
+++ b/solution.py
@@ -1,4 +1,3 @@
-import functools
 import math
 
 import jax
@@ -9,8 +8,26 @@
 from jax.sharding import PartitionSpec as P
 
 LANES = 128
-LINK_DTYPE = jnp.bfloat16
 NT_DIMS = (((1,), (1,)), ((), ()))
+
+CODE_STEPS = 1024.0
+CODE_LOW = -20.0
+
+
+def encode(value):
+    magnitude = jnp.abs(value)
+    exponent = jnp.floor(jnp.log(jnp.maximum(magnitude, 2.0**CODE_LOW)) * (1.0 / math.log(2.0)))
+    exponent = jnp.maximum(exponent, CODE_LOW)
+    code = jnp.round(((exponent - CODE_LOW) + magnitude * jnp.exp2(-exponent)) * CODE_STEPS)
+    return jnp.where(value < 0.0, -code, code).astype(jnp.int32).astype(jnp.int16)
+
+
+def decode(code):
+    level = code.astype(jnp.int32).astype(jnp.float32) * (1.0 / CODE_STEPS)
+    magnitude = jnp.abs(level)
+    octave = jnp.maximum(jnp.floor(magnitude), 1.0)
+    value = (magnitude - octave + 1.0) * jnp.exp2(octave + (CODE_LOW - 1.0))
+    return jnp.where(level < 0.0, -value, value)
 
 
 def split(value):
@@ -18,61 +35,63 @@
     return high, (value - high.astype(jnp.float32)).astype(jnp.bfloat16)
 
 
-def angle_factors(wavenumbers, lon_count):
-    coarse = jnp.arange(lon_count // LANES, dtype=jnp.int32) * LANES
-    fine = jnp.arange(LANES, dtype=jnp.int32)
-    steps = jnp.concatenate((coarse, fine))
-    phase = wavenumbers[:, None] * steps[None, :] % lon_count
+def dft_table(wave_order, lon_count, slot_count):
+    quarter = lon_count // 4
+    coarse_count = quarter // LANES
+    owners = wave_order.shape[0] // slot_count
+    steps = jnp.concatenate(
+        (jnp.arange(LANES, dtype=jnp.int32), jnp.arange(LANES, dtype=jnp.int32) % coarse_count * LANES)
+    )
+    phase = wave_order[:, None] * steps[None, :] % lon_count
     angles = phase.astype(jnp.float32) * (2.0 * math.pi / lon_count)
-    return jnp.cos(angles), jnp.sin(angles)
-
-
-def dft_table(wave_order, lon_count, slot_count):
-    cosine, sine = angle_factors(wave_order, lon_count)
-    coarse_count = lon_count // LANES
-    pad = -coarse_count % LANES
-    if pad:
-        fill = ((0, 0), (0, pad))
-        cosine = jnp.concatenate(
-            (jnp.pad(cosine[:, :coarse_count], fill), cosine[:, coarse_count:]), axis=1
-        )
-        sine = jnp.concatenate(
-            (jnp.pad(sine[:, :coarse_count], fill), sine[:, coarse_count:]), axis=1
-        )
-    owners = wave_order.shape[0] // slot_count
-    width = cosine.shape[1]
-    cosine = cosine.reshape(owners, slot_count, width)
-    sine = sine.reshape(owners, slot_count, width)
+    width = 2 * LANES
+    cosine = jnp.cos(angles).reshape(owners, slot_count, width)
+    sine = jnp.sin(angles).reshape(owners, slot_count, width)
+    turns = jnp.broadcast_to(
+        (wave_order % 4).astype(jnp.float32).reshape(owners, slot_count, 1), (owners, slot_count, LANES)
+    )
     step = 8
 
-    def body(cos_ref, sin_ref, out_ref):
+    def body(cos_ref, sin_ref, turn_ref, out_ref):
         @pl.loop(0, step)
         def _(owner):
             cos_all = cos_ref[owner]
             sin_all = sin_ref[owner]
-            cos_fine = cos_all[:, width - LANES :]
-            sin_fine = sin_all[:, width - LANES :]
-            row = pl.multiple_of(owner * 16, 16)
+            cos_fine = cos_all[:, :LANES]
+            sin_fine = sin_all[:, :LANES]
+            turn = turn_ref[owner]
+            turn = jnp.concatenate((turn, turn), axis=0)
+            one = jnp.ones_like(turn)
+            zero = jnp.zeros_like(turn)
+            keep = jnp.where(turn == 0.0, one, jnp.where(turn == 2.0, -one, zero)).astype(jnp.bfloat16)
+            swap = jnp.where(turn == 1.0, -one, jnp.where(turn == 3.0, one, zero)).astype(jnp.bfloat16)
+            opposite = jnp.where((turn == 1.0) | (turn == 3.0), -one, one).astype(jnp.bfloat16)
+            row = pl.multiple_of(owner * 2 * slot_count, 2 * slot_count)
             for a in range(coarse_count):
-                ca = cos_all[:, a : a + 1]
-                sa = sin_all[:, a : a + 1]
+                ca = cos_all[:, LANES + a : LANES + a + 1]
+                sa = sin_all[:, LANES + a : LANES + a + 1]
                 cosine_rows = ca * cos_fine - sa * sin_fine
                 sine_rows = sa * cos_fine + ca * sin_fine
-                out_ref[pl.ds(row, 16), a * LANES : (a + 1) * LANES] = jnp.concatenate(
-                    (cosine_rows, -sine_rows), axis=0
-                ).astype(jnp.bfloat16)
+                plain = jnp.concatenate((cosine_rows, -sine_rows), axis=0).astype(jnp.bfloat16)
+                other = jnp.concatenate((sine_rows, cosine_rows), axis=0).astype(jnp.bfloat16)
+                turned = plain * keep + other * swap
+                for index, value in enumerate((plain, turned, plain * opposite, turned * opposite)):
+                    start = index * quarter + a * LANES
+                    out_ref[pl.ds(row, 2 * slot_count), start : start + LANES] = value
 
     return pl.pallas_call(
         body,
         name="dft_table",
         grid=(owners // step,),
-        in_specs=[pl.BlockSpec((step, slot_count, width), lambda i: (i, 0, 0))] * 2,
-        out_specs=pl.BlockSpec((step * 16, lon_count), lambda i: (i, 0)),
-        out_shape=jax.ShapeDtypeStruct((owners * 16, lon_count), jnp.bfloat16),
+        in_specs=[pl.BlockSpec((step, slot_count, width), lambda i: (i, 0, 0))] * 2
+        + [pl.BlockSpec((step, slot_count, LANES), lambda i: (i, 0, 0))],
+        out_specs=pl.BlockSpec((step * 2 * slot_count, lon_count), lambda i: (i, 0)),
+        out_shape=jax.ShapeDtypeStruct((owners * 2 * slot_count, lon_count), jnp.bfloat16),
+        compiler_params=pltpu.CompilerParams(vmem_limit_bytes=8 << 20),
         cost_estimate=pl.CostEstimate(
             flops=owners * 16 * lon_count * 4, bytes_accessed=owners * 32 * lon_count, transcendentals=0
         ),
-    )(cosine, sine)
+    )(cosine, sine, turns)
 
 
 def transform_and_exchange(table, samples, scale):
@@ -149,7 +168,7 @@
                     preferred_element_type=jnp.float32,
                 )
                 total = term if total is None else total + term
-            send_ref[step] = (total * scale).astype(LINK_DTYPE).reshape(group, owner_rows, rows)
+            send_ref[step] = encode(total * scale).reshape(group, owner_rows, rows)
 
             @pl.when(step == 0)
             def _():
@@ -185,17 +204,17 @@
         name="transform_and_exchange",
         in_specs=[pl.BlockSpec(memory_space=pl.ANY), pl.BlockSpec(memory_space=pltpu.VMEM)],
         out_specs=pl.BlockSpec(memory_space=pl.ANY),
-        out_shape=jax.ShapeDtypeStruct((owners, owner_rows, rows), LINK_DTYPE),
+        out_shape=jax.ShapeDtypeStruct((owners, owner_rows, rows), jnp.int16),
         scratch_shapes=[
             pltpu.VMEM((2, block_rows, parts * length), jnp.bfloat16),
-            pltpu.VMEM((blocks, group, owner_rows, rows), LINK_DTYPE),
+            pltpu.VMEM((blocks, group, owner_rows, rows), jnp.int16),
             pltpu.SemaphoreType.DMA((2,)),
             pltpu.SemaphoreType.DMA,
             pltpu.SemaphoreType.DMA,
             pltpu.SemaphoreType.DMA,
         ],
         compiler_params=pltpu.CompilerParams(
-            collective_id=0, has_side_effects=True, vmem_limit_bytes=40 << 20
+            collective_id=0, has_side_effects=True, vmem_limit_bytes=20 << 20
         ),
     )(table, samples)
 
@@ -273,10 +292,9 @@
         for slot in range(slots):
             for parity in range(2):
                 for a in range(chunks):
-                    value = rows_ref[a, pl.ds(parity * slots + slot, block // 2, stride=2 * slots), :]
-                    high, low = split(value)
-                    out_ref[slot, parity, 0, :, lanes[a]] = high
-                    out_ref[slot, parity, 1, :, lanes[a]] = low
+                    out_ref[slot, parity, :, lanes[a]] = rows_ref[
+                        a, pl.ds(parity * slots + slot, block // 2, stride=2 * slots), :
+                    ].astype(jnp.bfloat16)
 
     return pl.pallas_call(
         body,
@@ -287,8 +305,8 @@
             pl.BlockSpec((slots, half), lambda i: (0, 0)),
             pl.BlockSpec((2, slots, half), lambda i: (0, 0, 0)),
         ],
-        out_specs=pl.BlockSpec((slots, 2, 2, block // 2, half), lambda i: (0, 0, 0, i, 0)),
-        out_shape=jax.ShapeDtypeStruct((slots, 2, 2, mode_count // 2, half), jnp.bfloat16),
+        out_specs=pl.BlockSpec((slots, 2, block // 2, half), lambda i: (0, 0, i, 0)),
+        out_shape=jax.ShapeDtypeStruct((slots, 2, mode_count // 2, half), jnp.bfloat16),
         scratch_shapes=[
             pltpu.VMEM((slots, half), jnp.float32),
             pltpu.VMEM((slots, half), jnp.float32),
@@ -298,23 +316,22 @@
         ],
         cost_estimate=pl.CostEstimate(
             flops=slots * half * mode_count * 10,
-            bytes_accessed=slots * half * mode_count * 4,
+            bytes_accessed=slots * half * mode_count * 2,
             transcendentals=0,
         ),
+        compiler_params=pltpu.CompilerParams(vmem_limit_bytes=8 << 20),
     )(wave_lanes, log_start, geometry)
 
 
 def project(received, legendre_table, field_order, belts, lons):
-    slots, _, _, half_modes, half = legendre_table.shape
-    sources = belts * lons
+    slots, _, half_modes, half = legendre_table.shape
     lat_local = 2 * half // belts
     items = received.shape[2] // lat_local
     levels = items * lons
     rows = 2 * levels
-    level_of = field_order.astype(jnp.int32)
     target = jnp.arange(2 * rows, dtype=jnp.int32)
     within = target % rows
-    source_level = jnp.take(level_of, within % levels)
+    source_level = jnp.take(field_order.astype(jnp.int32), within % levels)
     source_row = (source_level % items) * (2 * lons) + (source_level // items) * 2 + within // levels
     source_row = source_row + (target // rows) * rows
     order = (source_row[:, None] == jnp.arange(2 * rows, dtype=jnp.int32)[None, :]).astype(jnp.bfloat16)
@@ -322,49 +339,43 @@
         jnp.arange(lat_local)[:, None] + jnp.arange(lat_local)[None, :] == lat_local - 1
     ).astype(jnp.bfloat16)
 
-    def body(received_ref, table_ref, order_ref, mirror_ref, out_ref, wide_ref, sums_ref):
+    def body(received_ref, table_ref, order_ref, mirror_ref, out_ref, wide_ref):
         slot = pl.program_id(0)
         parity = pl.program_id(1)
 
         @pl.when((slot == 0) & (parity == 0))
         def _():
-            @pl.loop(0, belts)
+            @pl.loop(0, belts // 2)
             def _(belt):
-                for lon in range(lons):
-                    value = received_ref[belt * lons + lon].astype(jnp.float32)
-                    for item in range(items):
-                        wide_ref[belt, item, lon * 2 * slots : (lon + 1) * 2 * slots, :] = value[
-                            :, item * lat_local : (item + 1) * lat_local
-                        ]
-
-        @pl.when(parity == 0)
-        def _():
-            def rows_of(belt):
-                return jnp.concatenate(
-                    [wide_ref[belt, item, pl.ds(slot, 2 * lons, stride=slots), :] for item in range(items)],
+                other = belts - 1 - belt
+                for item in range(items):
+                    lanes = slice(item * lat_local, (item + 1) * lat_local)
+                    north = decode(received_ref[pl.ds(belt * lons, lons), :, lanes]).reshape(-1, lat_local)
+                    south = decode(received_ref[pl.ds(other * lons, lons), :, lanes]).reshape(-1, lat_local)
+                    high, low = split(south)
+                    south = jnp.dot(high, mirror_ref[...], preferred_element_type=jnp.float32) + jnp.dot(
+                        low, mirror_ref[...], preferred_element_type=jnp.float32
+                    )
+                    wide_ref[0, belt, item] = north + south
+                    wide_ref[1, belt, item] = north - south
+
+        value = jnp.concatenate(
+            [
+                jnp.concatenate(
+                    [
+                        wide_ref[parity, belt, item, pl.ds(slot, 2 * lons, stride=slots), :]
+                        for item in range(items)
+                    ],
                     axis=0,
                 )
-
-            for belt in range(belts // 2):
-                north = rows_of(belt)
-                south = jnp.dot(
-                    rows_of(belts - 1 - belt).astype(LINK_DTYPE),
-                    mirror_ref[...],
-                    preferred_element_type=jnp.float32,
-                )
-                for index, value in enumerate((north + south, north - south)):
-                    ordered = jnp.dot(
-                        order_ref[...],
-                        jnp.concatenate(split(value), axis=0),
-                        preferred_element_type=jnp.float32,
-                    )
-                    sums_ref[index, :, belt * lat_local : (belt + 1) * lat_local] = ordered.astype(jnp.bfloat16)
-
-        result = lax.dot_general(
-            sums_ref[parity], table_ref[0, 0, 0], NT_DIMS, preferred_element_type=jnp.float32
-        ) + lax.dot_general(
-            sums_ref[parity], table_ref[0, 0, 1], NT_DIMS, preferred_element_type=jnp.float32
+                for belt in range(belts // 2)
+            ],
+            axis=1,
         )
+        sums = jnp.dot(
+            order_ref[...], jnp.concatenate(split(value), axis=0), preferred_element_type=jnp.float32
+        ).astype(jnp.bfloat16)
+        result = lax.dot_general(sums, table_ref[0, 0], NT_DIMS, preferred_element_type=jnp.float32)
         out_ref[0] = result[:rows] + result[rows:]
 
     return pl.pallas_call(
@@ -373,17 +384,14 @@
         grid=(slots, 2),
         in_specs=[
             pl.BlockSpec(received.shape, lambda s, p: (0, 0, 0)),
-            pl.BlockSpec((1, 1, 2, half_modes, half), lambda s, p: (s, p, 0, 0, 0)),
+            pl.BlockSpec((1, 1, half_modes, half), lambda s, p: (s, p, 0, 0)),
             pl.BlockSpec((2 * rows, 2 * rows), lambda s, p: (0, 0)),
             pl.BlockSpec((lat_local, lat_local), lambda s, p: (0, 0)),
         ],
         out_specs=pl.BlockSpec((1, rows, half_modes), lambda s, p: (s, 0, p)),
         out_shape=jax.ShapeDtypeStruct((slots, rows, 2 * half_modes), jnp.float32),
-        scratch_shapes=[
-            pltpu.VMEM((belts, items, 2 * lons * slots, lat_local), jnp.float32),
-            pltpu.VMEM((2, 2 * rows, half), jnp.bfloat16),
-        ],
-        compiler_params=pltpu.CompilerParams(vmem_limit_bytes=40 << 20),
+        scratch_shapes=[pltpu.VMEM((2, belts // 2, items, 2 * lons * slots, lat_local), jnp.float32)],
+        compiler_params=pltpu.CompilerParams(vmem_limit_bytes=20 << 20),
     )(received, legendre_table, order, mirror)
 
 

time: 148 us -> 134 us (0.905)
  Pallas kernels: 126 us -> 97.6 us
  local copies, waits for them, and re-layouts: 5.32 us -> 21.7 us
  other arithmetic: 7.32 us -> 4.85 us
    pallas_call x1, Pallas kernels: 32.1 us -> 12.3 us  [project(): pl.pallas_call(body, name='project', grid=(slots, 2), in_specs=[pl.BlockS...]
    unnamed x8 -> x12, local copies, waits for them, and re-layouts: 0.02 us -> 17.2 us
    pallas_call x1, Pallas kernels: 24.6 us -> 13.1 us  [dft_table(): pl.pallas_call(body, name='dft_table', grid=(owners // step,), in_specs=[...]
    pallas_call x1, Pallas kernels: 41.1 us -> 51 us  [transform_and_exchange(): pl.pallas_call(body, name='transform_and_exchange', in_specs=[pl.BlockSpe...]
    pallas_call x1, Pallas kernels: 28.2 us -> 21.3 us  [legendre(): pl.pallas_call(body, name='legendre', grid=(mode_count // block,), in_spe...]
  transfers between devices with their start and end apart: 1 -> 1, of which waited for: 0 -> 0; matrix products, arithmetic and copies ran while one was open for 7% -> 5% of each run, Pallas kernels for 36% -> 26%
where the time goes in v2:
time: 134 us; the launch traced here: 133 us
  Pallas kernels  97.6 us (73%)
  local copies, waits for them, and re-layouts  21.7 us (16%)
  starting transfers between devices  8.45 us (6%)
  other arithmetic  4.85 us (4%)
    pallas_call x1, Pallas kernels, transform_and_exchange(): pl.pallas_call(body, name='transform_and_exchange', in_specs=[pl.BlockSpe...  51 us
    pallas_call x1, Pallas kernels, legendre(): pl.pallas_call(body, name='legendre', grid=(mode_count // block,), in_spe...  21.3 us
    unnamed x12, local copies, waits for them, and re-layouts  17.2 us
    pallas_call x1, Pallas kernels, dft_table(): pl.pallas_call(body, name='dft_table', grid=(owners // step,), in_specs=[...  13.1 us
    pallas_call x1, Pallas kernels, project(): pl.pallas_call(body, name='project', grid=(slots, 2), in_specs=[pl.BlockS...  12.3 us
    all_to_all x1, starting transfers between devices, on_device(): lax.all_to_all(blocks, 'lon', split_axis=0, concat_axis=0, tiled=True)  8.45 us
    sin x1, other arithmetic, dft_table(): sine = jnp.sin(angles).reshape(owners, slot_count, width)  4.15 us
    reshape x1, local copies, waits for them, and re-layouts, on_device(): return spectral.reshape(slots, 2, levels, 2, mode_count // 2)  2.78 us
  transfers between devices with their start and end apart: 1, of which 0 were waited for; matrix products, arithmetic and copies ran while one was open for 5% of the time, Pallas kernels for 26%

profile of v2, /device:TPU:1, one launch (start us, length us, event | category | flops | bytes accessed | tf_op | source)
XLA Modules:
  0.0 132.8 jit_solution(11802305226498740432)
XLA Ops:
  0.0 0.0 copy-start
  0.0 0.0 copy-start.5
  0.0 8.5 %all-to-all-start = ((bf16[8,512,512]{2,1,0:T(8,128)(2,1)}), bf16[8,512,512]{2,1,0:T(8,128)(2,1)}, u32[]{:S(2)}, u32[]{:S(2)}) async-start(bf16[8,512,512]{2,1,0:T(8,128)(2,1)} %bitcast.3), calls=%async_computation | async-start | bytes 8388608 | tf_op jit(solution)/shard_map/all_to_all | solution.py:408
  8.5 0.0 copy-done.5
  8.5 0.1 mul.104
  8.6 0.1 broadcast_in_dim.22
  8.7 4.1 %fusion.3 = (f32[128,8,256]{2,1,0:T(8,128)S(1)}, f32[128,8,256]{2,1,0:T(8,128)S(1)}) fusion(s32[256]{0:T(256)S(1)} %pad_add_fusion, s32[128,8]{1,0:T(8,128)S(1)} %mul.104), kind=kLoop, calls=%fused_computation.9 | loop fusion | flops 3670016 | bytes 2102272 | tf_op jit(solution)/shard_map/sin | solution.py:49
  12.8 0.2 broadcast_in_dim.23.turn_ref
  13.0 13.1 %dft_table.1.table_ref = bf16[2048,4096]{1,0:T(8,128)(2,1)S(1)} custom-call(f32[128,8,256]{2,1,0:T(8,128)S(1)} %get-tuple-element.10.cos_ref, f32[128,8,256]{2,1,0:T(8,128)S(1)} %get-tuple-element.9.sin_ref, f32[128,8,128]{2,1,0:T(8,128)S(1)} %broadcast_in_dim.23.turn_ref), custom_call_target="tpu_custom_call" | custom-call | flops 33554432 | bytes 16777216 | tf_op jit(solution)/shard_map/dft_table/pallas_call | solution.py:82
  26.2 0.0 copy-start.3
  26.2 5.7 %copy-done.3 = bf16[2048,4096]{1,0:T(8,128)(2,1)} copy-done((bf16[2048,4096]{1,0:T(8,128)(2,1)}, bf16[2048,4096]{1,0:T(8,128)(2,1)S(1)}, u32[]{:S(2)}) %copy-start.3) | copy-done | bytes 16777240
  31.9 0.1 dynamic-slice_convert_fusion
  32.0 0.1 sine_multiply_fusion
  32.2 0.2 select_reduce_fusion
  32.4 0.1 multiply_add_fusion.log_ref
  32.5 0.1 broadcast_in_dim.26.wave_ref
  32.5 21.3 %legendre.1.table_ref = bf16[8,2,512,1024]{3,2,1,0:T(8,128)(2,1)S(1)} custom-call(f32[8,128]{1,0:T(8,128)S(1)} %broadcast_in_dim.26.wave_ref, f32[8,1024]{1,0:T(8,128)S(1)} %multiply_add_fusion.log_ref, f32[2,8,1024]{2,1,0:T(8,128)S(1)} %mul.119.geo_ref), custom_call_target="tpu_custom_call" | custom-call | flops 83886080 | bytes 16777216 | tf_op jit(solution)/shard_map/legendre/pallas_call | solution.py:299
  53.8 0.0 copy-start.1
  53.8 5.7 %copy-done.1 = bf16[8,2,512,1024]{3,2,1,0:T(8,128)(2,1)} copy-done((bf16[8,2,512,1024]{3,2,1,0:T(8,128)(2,1)}, bf16[8,2,512,1024]{3,2,1,0:T(8,128)(2,1)S(1)}, u32[]{:S(2)}) %copy-start.1) | copy-done | bytes 16777240
  59.6 0.0 copy-done
  59.6 1.2 gather_fusion
  60.8 0.1 fusion.5
  60.9 0.0 all-to-all-done.samples_ref
  60.9 0.0 copy-start.4
  60.9 5.8 %copy-done.4 = bf16[2048,4096]{1,0:T(8,128)(2,1)S(1)} copy-done((bf16[2048,4096]{1,0:T(8,128)(2,1)S(1)}, bf16[2048,4096]{1,0:T(8,128)(2,1)}, u32[]{:S(2)}) %copy-start.4) | copy-done | bytes 16777240
  66.7 0.0 copy-start.2
  66.7 51.0 %transform_and_exchange.1.received_ref = s16[128,16,512]{2,1,0:T(8,128)(2,1)S(1)} custom-call(bf16[2048,4096]{1,0:T(8,128)(2,1)S(1)} %copy-done.4, bf16[8,512,512]{2,1,0:T(8,128)(2,1)} %all-to-all-done.samples_ref), custom_call_target="tpu_custom_call" | custom-call | tf_op jit(solution)/shard_map/transform_and_exchange/pallas_call | solution.py:202
  117.7 0.0 copy-done.2
  117.7 12.3 %project.1 = f32[8,64,1024]{2,1,0:T(8,128)S(1)} custom-call(s16[128,16,512]{2,1,0:T(8,128)(2,1)S(1)} %transform_and_exchange.1.received_ref, bf16[8,2,512,1024]{3,2,1,0:T(8,128)(2,1)S(1)} %copy-done.2, bf16[128,128]{1,0:T(8,128)(2,1)S(1)} %get-tuple-element.13.order_ref, bf16[128,128]{1,0:T(8,128)(2,1)S(1)} %get-tuple-element.14.mirror_ref), custom_call_target="tpu_custom_call" | custom-call | tf_op jit(solution)/shard_map/project/pallas_call | solution.py:381
  130.0 2.8 %reshape.209 = f32[8,2,32,2,512]{4,3,2,1,0:T(2,128)} reshape(f32[8,64,1024]{2,1,0:T(8,128)S(1)} %project.1) | data formatting | bytes 4194304 | tf_op jit(solution)/shard_map/reshape | solution.py:416
  (13 shorter events, 0.1 us)
Async XLA Ops:
  0.0 59.6 %copy-start = (s32[32]{0:T(128)S(1)}, s32[32]{0:T(128)}, u32[]{:S(2)}) copy-start(s32[32]{0:T(128)} %param.4) | copy-start | bytes 388
  0.0 8.5 %copy-start.5 = (s32[1024]{0:T(1024)S(1)}, s32[1024]{0:T(1024)}, u32[]{:S(2)}) copy-start(s32[1024]{0:T(1024)} %param.5) | copy-start | bytes 12292
  0.0 60.9 %all-to-all-start = ((bf16[8,512,512]{2,1,0:T(8,128)(2,1)}), bf16[8,512,512]{2,1,0:T(8,128)(2,1)}, u32[]{:S(2)}, u32[]{:S(2)}) async-start(bf16[8,512,512]{2,1,0:T(8,128)(2,1)} %bitcast.3), calls=%async_computation | async-start | bytes 8388608 | tf_op jit(solution)/shard_map/all_to_all | solution.py:408
  26.2 5.7 %copy-start.3 = (bf16[2048,4096]{1,0:T(8,128)(2,1)}, bf16[2048,4096]{1,0:T(8,128)(2,1)S(1)}, u32[]{:S(2)}) copy-start(bf16[2048,4096]{1,0:T(8,128)(2,1)S(1)} %dft_table.1.table_ref) | copy-start | bytes 50331652
  53.8 5.7 %copy-start.1 = (bf16[8,2,512,1024]{3,2,1,0:T(8,128)(2,1)}, bf16[8,2,512,1024]{3,2,1,0:T(8,128)(2,1)S(1)}, u32[]{:S(2)}) copy-start(bf16[8,2,512,1024]{3,2,1,0:T(8,128)(2,1)S(1)} %legendre.1.table_ref) | copy-start | bytes 50331652
  60.9 5.8 %copy-start.4 = (bf16[2048,4096]{1,0:T(8,128)(2,1)S(1)}, bf16[2048,4096]{1,0:T(8,128)(2,1)}, u32[]{:S(2)}) copy-start(bf16[2048,4096]{1,0:T(8,128)(2,1)} %copy-done.3) | copy-start | bytes 50331652
  66.7 51.0 %copy-start.2 = (bf16[8,2,512,1024]{3,2,1,0:T(8,128)(2,1)S(1)}, bf16[8,2,512,1024]{3,2,1,0:T(8,128)(2,1)}, u32[]{:S(2)}) copy-start(bf16[8,2,512,1024]{3,2,1,0:T(8,128)(2,1)} %copy-done.1) | copy-start | bytes 50331652

commit v3 on v2

--- a/solution.py
+++ b/solution.py
@@ -87,7 +87,6 @@
         + [pl.BlockSpec((step, slot_count, LANES), lambda i: (i, 0, 0))],
         out_specs=pl.BlockSpec((step * 2 * slot_count, lon_count), lambda i: (i, 0)),
         out_shape=jax.ShapeDtypeStruct((owners * 2 * slot_count, lon_count), jnp.bfloat16),
-        compiler_params=pltpu.CompilerParams(vmem_limit_bytes=8 << 20),
         cost_estimate=pl.CostEstimate(
             flops=owners * 16 * lon_count * 4, bytes_accessed=owners * 32 * lon_count, transcendentals=0
         ),
@@ -214,7 +213,7 @@
             pltpu.SemaphoreType.DMA,
         ],
         compiler_params=pltpu.CompilerParams(
-            collective_id=0, has_side_effects=True, vmem_limit_bytes=20 << 20
+            collective_id=0, has_side_effects=True, vmem_limit_bytes=40 << 20
         ),
     )(table, samples)
 
@@ -319,7 +318,6 @@
             bytes_accessed=slots * half * mode_count * 2,
             transcendentals=0,
         ),
-        compiler_params=pltpu.CompilerParams(vmem_limit_bytes=8 << 20),
     )(wave_lanes, log_start, geometry)
 
 

time: 134 us -> 134 us (level)
  local copies, waits for them, and re-layouts: 21.7 us -> 12.2 us
  Pallas kernels: 97.6 us -> 104 us
  other arithmetic: 4.85 us -> 7.09 us
    unnamed x12 -> x6, local copies, waits for them, and re-layouts: 17.2 us -> 5.77 us
    pallas_call x1, Pallas kernels: 13.1 us -> 16.8 us  [dft_table(): pl.pallas_call(body, name='dft_table', grid=(owners // step,), in_specs=[...]
    pallas_call x1, Pallas kernels: 21.3 us -> 23.9 us  [legendre(): pl.pallas_call(body, name='legendre', grid=(mode_count // block,), in_spe...]
    sin x1, other arithmetic: 4.15 us -> 5.78 us  [dft_table(): sine = jnp.sin(angles).reshape(owners, slot_count, width)]
  transfers between devices with their start and end apart: 1 -> 1, of which waited for: 0 -> 0; matrix products, arithmetic and copies ran while one was open for 5% -> 8% of each run, Pallas kernels for 26% -> 31%
where the time goes in v3:
time: 134 us; the launch traced here: 132 us
  Pallas kernels  104 us (78%)
  local copies, waits for them, and re-layouts  12.2 us (9%)
  starting transfers between devices  8.45 us (6%)
  other arithmetic  7.09 us (5%)
    pallas_call x1, Pallas kernels, transform_and_exchange(): pl.pallas_call(body, name='transform_and_exchange', in_specs=[pl.BlockSpe...  50.9 us
    pallas_call x1, Pallas kernels, legendre(): pl.pallas_call(body, name='legendre', grid=(mode_count // block,), in_spe...  23.9 us
    pallas_call x1, Pallas kernels, dft_table(): pl.pallas_call(body, name='dft_table', grid=(owners // step,), in_specs=[...  16.8 us
    pallas_call x1, Pallas kernels, project(): pl.pallas_call(body, name='project', grid=(slots, 2), in_specs=[pl.BlockS...  12.3 us
    all_to_all x1, starting transfers between devices, on_device(): lax.all_to_all(blocks, 'lon', split_axis=0, concat_axis=0, tiled=True)  8.45 us
    sin x1, other arithmetic, dft_table(): sine = jnp.sin(angles).reshape(owners, slot_count, width)  5.78 us
    unnamed x6, local copies, waits for them, and re-layouts  5.77 us
    reshape x1, local copies, waits for them, and re-layouts, on_device(): return spectral.reshape(slots, 2, levels, 2, mode_count // 2)  2.78 us
  transfers between devices with their start and end apart: 1, of which 0 were waited for; matrix products, arithmetic and copies ran while one was open for 8% of the time, Pallas kernels for 31%

profile of v3, /device:TPU:1, one launch (start us, length us, event | category | flops | bytes accessed | tf_op | source)
XLA Modules:
  0.0 131.8 jit_solution(11918211565946649870)
XLA Ops:
  0.0 0.0 copy-start
  0.0 0.0 copy-start.2
  0.0 8.5 %all-to-all-start = ((bf16[8,512,512]{2,1,0:T(8,128)(2,1)}), bf16[8,512,512]{2,1,0:T(8,128)(2,1)}, u32[]{:S(2)}, u32[]{:S(2)}) async-start(bf16[8,512,512]{2,1,0:T(8,128)(2,1)} %bitcast.3), calls=%async_computation | async-start | bytes 8388608 | tf_op jit(solution)/shard_map/all_to_all | solution.py:406
  8.5 0.0 copy-done.2
  8.5 0.1 mul.104
  8.6 0.1 broadcast_in_dim.22
  8.7 5.8 %fusion.3 = (f32[128,8,256]{2,1,0:T(8,128)}, f32[128,8,256]{2,1,0:T(8,128)}) fusion(s32[256]{0:T(256)S(1)} %pad_add_fusion, s32[128,8]{1,0:T(8,128)S(1)} %mul.104), kind=kLoop, calls=%fused_computation.9 | loop fusion | flops 3670016 | bytes 2102272 | tf_op jit(solution)/shard_map/sin | solution.py:49
  14.5 1.0 broadcast_in_dim.23.turn_ref
  15.5 16.8 %dft_table.1.table_ref = bf16[2048,4096]{1,0:T(8,128)(2,1)} custom-call(f32[128,8,256]{2,1,0:T(8,128)} %get-tuple-element.10.cos_ref, f32[128,8,256]{2,1,0:T(8,128)} %get-tuple-element.9.sin_ref, f32[128,8,128]{2,1,0:T(8,128)} %broadcast_in_dim.23.turn_ref), custom_call_target="tpu_custom_call" | custom-call | flops 33554432 | bytes 16777216 | tf_op jit(solution)/shard_map/dft_table/pallas_call | solution.py:82
  32.3 0.1 dynamic-slice_convert_fusion
  32.4 0.1 sine_multiply_fusion
  32.6 0.2 select_reduce_fusion
  32.8 0.7 multiply_add_fusion.log_ref
  33.5 0.7 broadcast_in_dim.26.wave_ref
  34.1 0.6 mul.119.geo_ref
  34.8 23.9 %legendre.1.table_ref = bf16[8,2,512,1024]{3,2,1,0:T(8,128)(2,1)} custom-call(f32[8,128]{1,0:T(8,128)} %broadcast_in_dim.26.wave_ref, f32[8,1024]{1,0:T(8,128)} %multiply_add_fusion.log_ref, f32[2,8,1024]{2,1,0:T(8,128)} %mul.119.geo_ref), custom_call_target="tpu_custom_call" | custom-call | flops 83886080 | bytes 16777216 | tf_op jit(solution)/shard_map/legendre/pallas_call | solution.py:298
  58.7 0.0 copy-done
  58.7 1.2 gather_fusion
  60.0 0.1 fusion.5
  60.1 0.0 all-to-all-done.samples_ref
  60.1 50.9 %transform_and_exchange.1.received_ref = s16[128,16,512]{2,1,0:T(8,128)(2,1)S(1)} custom-call(bf16[2048,4096]{1,0:T(8,128)(2,1)} %dft_table.1.table_ref, bf16[8,512,512]{2,1,0:T(8,128)(2,1)} %all-to-all-done.samples_ref), custom_call_target="tpu_custom_call" | custom-call | tf_op jit(solution)/shard_map/transform_and_exchange/pallas_call | solution.py:201
  110.9 0.0 copy-start.1
  111.0 5.8 %copy-done.1 = bf16[8,2,512,1024]{3,2,1,0:T(8,128)(2,1)S(1)} copy-done((bf16[8,2,512,1024]{3,2,1,0:T(8,128)(2,1)S(1)}, bf16[8,2,512,1024]{3,2,1,0:T(8,128)(2,1)}, u32[]{:S(2)}) %copy-start.1) | copy-done | bytes 16777240
  116.7 12.3 %project.1 = f32[8,64,1024]{2,1,0:T(8,128)S(1)} custom-call(s16[128,16,512]{2,1,0:T(8,128)(2,1)S(1)} %transform_and_exchange.1.received_ref, bf16[8,2,512,1024]{3,2,1,0:T(8,128)(2,1)S(1)} %copy-done.1, bf16[128,128]{1,0:T(8,128)(2,1)S(1)} %get-tuple-element.13.order_ref, bf16[128,128]{1,0:T(8,128)(2,1)S(1)} %get-tuple-element.14.mirror_ref), custom_call_target="tpu_custom_call" | custom-call | tf_op jit(solution)/shard_map/project/pallas_call | solution.py:379
  129.0 2.8 %reshape.209 = f32[8,2,32,2,512]{4,3,2,1,0:T(2,128)} reshape(f32[8,64,1024]{2,1,0:T(8,128)S(1)} %project.1) | data formatting | bytes 4194304 | tf_op jit(solution)/shard_map/reshape | solution.py:414
  (12 shorter events, 0.1 us)
Async XLA Ops:
  0.0 58.7 %copy-start = (s32[32]{0:T(128)S(1)}, s32[32]{0:T(128)}, u32[]{:S(2)}) copy-start(s32[32]{0:T(128)} %param.4) | copy-start | bytes 388
  0.0 8.5 %copy-start.2 = (s32[1024]{0:T(1024)S(1)}, s32[1024]{0:T(1024)}, u32[]{:S(2)}) copy-start(s32[1024]{0:T(1024)} %param.5) | copy-start | bytes 12292
  0.0 60.1 %all-to-all-start = ((bf16[8,512,512]{2,1,0:T(8,128)(2,1)}), bf16[8,512,512]{2,1,0:T(8,128)(2,1)}, u32[]{:S(2)}, u32[]{:S(2)}) async-start(bf16[8,512,512]{2,1,0:T(8,128)(2,1)} %bitcast.3), calls=%async_computation | async-start | bytes 8388608 | tf_op jit(solution)/shard_map/all_to_all | solution.py:406
  110.9 5.8 %copy-start.1 = (bf16[8,2,512,1024]{3,2,1,0:T(8,128)(2,1)S(1)}, bf16[8,2,512,1024]{3,2,1,0:T(8,128)(2,1)}, u32[]{:S(2)}) copy-start(bf16[8,2,512,1024]{3,2,1,0:T(8,128)(2,1)} %legendre.1.table_ref) | copy-start | bytes 50331652
